TPU v7x, 32 devices: a whole 2x2x4 slice. The times are simulated.
32 devices in a mesh: dp: 8 (over z, x), rep: 4 (over y, core).
Axes of the slice: x: 2, y: 2, z: 4, core: 2. Of those that a mesh axis runs over, the one named last changes fastest.
Arguments:
- hot_ids: int32 [8192, 2], P(('dp', 'rep')), may hold values from 0 to 1023
- cold_owner: int32 [16384, 1], P(('dp', 'rep')), may hold values from 0 to 7; in each aligned block of 512 rows (0 to 511, 512 to 1023, ...) at most 128 rows name the same one
- cold_offset: int32 [16384], P(('dp', 'rep')), may hold values from 0 to 511
- labels: int32 [8192], P(('dp', 'rep')), may hold values 0 or 1
- top_weight: bfloat16 [512, 1024], replicated, may hold values from -0.25 to 0.25
- out_weight: float32 [1024], replicated, may hold values from -0.5 to 0.5
- cold_table: float32 [4096, 128], P('dp'), may hold values from -6 to 6
- cold_accum: float32 [4096, 128], P('dp'), may hold values from 0.0001 to 0.01
- hot_cache: float32 [1024, 128], replicated, may hold values from -6 to 6
- hot_accum: float32 [1024, 128], replicated, may hold values from 0.01 to 1
- pending: float32 [32768, 128], P(('dp', 'rep')), may hold values from -0.3 to 0.3
- refresh_blocks: int32 [3], replicated, may hold values from 0 to 7, as said below
- block_clock: int32 [8], replicated, may hold values from 0 to 8
Outputs:
- cold_table_new: float32 [4096, 128], P('dp')
- cold_accum_new: float32 [4096, 128], P('dp')
- hot_cache_new: float32 [1024, 128], replicated
- hot_accum_new: float32 [1024, 128], replicated
- pending_new: float32 [32768, 128], P(('dp', 'rep'))
- top_grad: float32 [512, 1024], P(('dp', 'rep'))
- out_grad: float32 [1024], replicated
Inputs may be any that keep to these rules, and one draw needn't show every extreme that they name: `cold_owner`: within the lookups of one device (512 rows), no owner is named more than 128 times. `refresh_blocks`: the block numbers are distinct.
All inputs are finite; a program needn't handle non-finite values. No bound on the sum of `labels` on one device may be relied on, other than what follows from the above.
Results may differ from a plain program's by a relative error of at most 0.00165.
The roundings to bfloat16 on the way count: a program that leaves them out, or rounds other values in their place, can miss the bound.
Values may be sent and summed in bfloat16 or wider, within the bound.
A program may use at most 64 MiB of HBM per device.

v0:
```python
import jax
import jax.numpy as jnp
from jax import lax
from jax.sharding import PartitionSpec as P

BLOCK = 128


step_size = 0.5
epsilon = 1e-08


def adagrad(table_rows, accum_rows, gradient):
    accum_next = accum_rows + gradient * gradient
    return (table_rows - step_size * gradient / (jnp.sqrt(accum_next) + epsilon), accum_next)


def local(
    hot_ids,
    cold_owner,
    cold_offset,
    labels,
    top_weight,
    out_weight,
    cold_table,
    cold_accum,
    hot_cache,
    hot_accum,
    pending,
    refresh_blocks,
    block_clock,
):
    width = hot_cache.shape[1]
    samples = hot_ids.shape[0]
    hot_feats = hot_ids.shape[1]
    lookups = cold_offset.shape[0]
    cold_feats = lookups // samples
    owners_count = lax.axis_size("dp")
    capacity = max(2, 2 * lookups // owners_count)
    owners = cold_owner[:, 0]
    matches = (owners[:, None] == jnp.arange(owners_count, dtype=jnp.int32)[None, :]).astype(
        jnp.int32
    )
    earlier = jnp.cumsum(matches, axis=0) - matches
    positions = jnp.sum(earlier * matches, axis=1)
    targets = owners * capacity + positions
    requests = jnp.zeros((owners_count * capacity,), jnp.int32).at[targets].set(cold_offset)
    requests = requests.reshape(owners_count, capacity)
    asked = lax.all_to_all(requests, "dp", split_axis=0, concat_axis=0, tiled=True)
    found = cold_table[asked].astype(jnp.bfloat16)
    returned = lax.all_to_all(found, "dp", split_axis=0, concat_axis=0, tiled=True)
    cold_rows = returned.reshape(owners_count * capacity, width)[targets]
    cold_rows = cold_rows.reshape(samples, cold_feats, width)
    hot_rows = hot_cache[hot_ids].astype(jnp.bfloat16)
    inputs = jnp.concatenate([hot_rows, cold_rows], axis=1).reshape(
        samples, (hot_feats + cold_feats) * width
    )
    preact = jnp.dot(inputs, top_weight, preferred_element_type=jnp.float32)
    hidden = jax.nn.silu(preact).astype(jnp.bfloat16)
    hidden_wide = hidden.astype(jnp.float32)
    logits = jnp.dot(hidden_wide, out_weight, precision=lax.Precision.HIGHEST)
    errors = jax.nn.sigmoid(logits) - labels.astype(jnp.float32)
    gates = jax.nn.sigmoid(preact)
    slope = gates * (1.0 + preact * (1.0 - gates))
    dhidden = (errors[:, None] * out_weight[None, :] * slope).astype(jnp.bfloat16)
    head_term = jnp.dot(errors, hidden_wide, precision=lax.Precision.HIGHEST)
    top_grad = lax.psum_scatter(
        lax.dot_general(
            inputs, dhidden, (((0,), (0,)), ((), ())), preferred_element_type=jnp.float32
        ),
        ("dp", "rep"),
        scatter_dimension=0,
        tiled=True,
    )
    dinputs = lax.dot_general(
        dhidden, top_weight, (((1,), (1,)), ((), ())), preferred_element_type=jnp.float32
    ).astype(jnp.bfloat16)
    dinputs = dinputs.reshape(samples, hot_feats + cold_feats, width)
    cold_dx = dinputs[:, hot_feats:].reshape(lookups, width)
    outgoing = jnp.zeros((owners_count * capacity, width), jnp.bfloat16).at[targets].set(cold_dx)
    outgoing = outgoing.reshape(owners_count, capacity, width)
    incoming = lax.all_to_all(outgoing, "dp", split_axis=0, concat_axis=0, tiled=True)
    own_rows = cold_table.shape[0]
    cold_grad = (
        jnp.zeros((own_rows, width), jnp.float32)
        .at[asked.reshape(-1)]
        .add(incoming.reshape(-1, width).astype(jnp.float32))
    )
    quarter = own_rows // lax.axis_size("rep")
    offset_rows = lax.axis_index("rep") * quarter
    cold_share = lax.psum_scatter(cold_grad, "rep", scatter_dimension=0, tiled=True)
    table_share = lax.dynamic_slice_in_dim(cold_table, offset_rows, quarter, 0)
    accum_share = lax.dynamic_slice_in_dim(cold_accum, offset_rows, quarter, 0)
    table_updated, accum_updated = adagrad(table_share, accum_share, cold_share)
    cold_table_new, cold_accum_new = (
        lax.all_gather(table_updated, "rep", axis=0, tiled=True),
        lax.all_gather(accum_updated, "rep", axis=0, tiled=True),
    )
    hot_count = hot_cache.shape[0]
    blocks_count = hot_count // BLOCK
    hot_dx = dinputs[:, :hot_feats].reshape(samples * hot_feats, width).astype(jnp.float32)
    hot_grad = jnp.zeros((hot_count, width), jnp.float32).at[hot_ids.reshape(-1)].add(hot_dx)
    carried = (pending + hot_grad).reshape(blocks_count, BLOCK, width)
    picked = carried[refresh_blocks]
    divisors = 1.0 + block_clock[refresh_blocks].astype(jnp.float32)
    cache_blocks = hot_cache.reshape(blocks_count, BLOCK, width)
    accum_blocks = hot_accum.reshape(blocks_count, BLOCK, width)
    cache_chosen = cache_blocks[refresh_blocks]
    accum_chosen = accum_blocks[refresh_blocks]
    picked_sum, out_grad = lax.psum((picked, head_term), ("dp", "rep"))
    flush = picked_sum / divisors[:, None, None]
    cache_part, accum_part = adagrad(cache_chosen, accum_chosen, flush)
    hot_cache_new = cache_blocks.at[refresh_blocks].set(cache_part).reshape(hot_count, width)
    hot_accum_new = accum_blocks.at[refresh_blocks].set(accum_part).reshape(hot_count, width)
    pending_new = carried.at[refresh_blocks].set(0.0).reshape(hot_count, width)
    return (
        cold_table_new,
        cold_accum_new,
        hot_cache_new,
        hot_accum_new,
        pending_new,
        top_grad,
        out_grad,
    )


def solution(mesh):
    in_specs = (
        P(("dp", "rep"), None),
        P(("dp", "rep"), None),
        P(("dp", "rep")),
        P(("dp", "rep")),
        P(),
        P(),
        P("dp", None),
        P("dp", None),
        P(),
        P(),
        P(("dp", "rep"), None),
        P(),
        P(),
    )
    out_specs = (
        P("dp", None),
        P("dp", None),
        P(),
        P(),
        P(("dp", "rep"), None),
        P(("dp", "rep"), None),
        P(),
    )
    return jax.shard_map(local, mesh=mesh, in_specs=in_specs, out_specs=out_specs, check_vma=False)
```

profile of v0, /device:TPU:0, one launch (start us, length us, event | category | flops | bytes accessed | tf_op | source)
XLA Modules:
  0.0 245.3 jit_solution(7436814418134962637)
XLA Ops:
  10.9 2.6 %scatter_custom_fusion = s32[1024]{0:T(1024)S(1)} fusion(s32[512]{0:T(512)S(1)} %bitcast.83, s32[512]{0:T(512)} %param.15, s32[]{:T(128)} %constant.13.clone.1), kind=kCustom, calls=%fused_computation.55 | custom fusion | bytes 4608 | tf_op jit(solution)/shard_map/scatter | solution.py:47
  13.5 13.6 %all_to_all.22 = s32[8,1,128]{2,1,0:T(1,128)S(1)} all-to-all(s32[8,1,128]{2,1,0:T(1,128)S(1)} %bitcast.82), channel_id=1, replica_groups=mesh['dp'=8,'rep'=4] {'dp'}, dimensions={0} | all-to-all | bytes 8192 | tf_op jit(solution)/shard_map/all_to_all | solution.py:49
  27.1 4.1 %gather_fusion.1 = bf16[1024,128]{1,0:T(8,128)(2,1)} fusion(f32[512,128]{1,0:T(8,128)S(1)} %copy-done.2, s32[1024]{0:T(1024)S(1)} %fusion.17), kind=kCustom, calls=%fused_computation.1 | custom fusion | bytes 528384 | tf_op jit(solution)/shard_map/gather | solution.py:50
  31.2 3.4 %all-to-all-start.1 = ((bf16[8,128,128]{2,1,0:T(8,128)(2,1)}), bf16[8,128,128]{2,1,0:T(8,128)(2,1)S(1)}, u32[]{:S(2)}, u32[]{:S(2)}) async-start(bf16[8,128,128]{2,1,0:T(8,128)(2,1)} %bitcast.12), calls=%async_computation.1 | async-start | bytes 524288 | tf_op jit(solution)/shard_map/all_to_all | solution.py:51
  36.6 6.2 %all-to-all-done.1 = bf16[8,128,128]{2,1,0:T(8,128)(2,1)S(1)} async-done(((bf16[8,128,128]{2,1,0:T(8,128)(2,1)}), bf16[8,128,128]{2,1,0:T(8,128)(2,1)S(1)}, u32[]{:S(2)}, u32[]{:S(2)}) %all-to-all-start.1) | async-done | bytes 262176 | tf_op jit(solution)/shard_map/all_to_all | solution.py:51
  42.8 1.3 gather_fusion.2
  46.3 1.3 convolution_convert_fusion
  47.6 1.8 reshape.179
  49.4 1.9 fusion.20
  51.3 2.8 %scatter_custom_fusion.1 = bf16[1024,128]{1,0:T(8,128)(2,1)} fusion(s32[512]{0:T(512)S(1)} %bitcast.85, bf16[512,128]{1,0:T(8,128)(2,1)} %bitcast.77, bf16[]{:T(256)} %constant.17.clone.1), kind=kCustom, calls=%fused_computation.31 | custom fusion | bytes 262656 | tf_op jit(solution)/shard_map/scatter | solution.py:80
  54.1 4.0 %all-to-all-start.2 = ((bf16[8,128,128]{2,1,0:T(8,128)(2,1)}), bf16[8,128,128]{2,1,0:T(8,128)(2,1)}, u32[]{:S(2)}, u32[]{:S(2)}) async-start(bf16[8,128,128]{2,1,0:T(8,128)(2,1)} %bitcast.71), calls=%async_computation.2 | async-start | bytes 524288 | tf_op jit(solution)/shard_map/all_to_all | solution.py:82
  60.6 3.6 %scatter_custom_fusion.3 = f32[1024,128]{1,0:T(8,128)S(1)} fusion(f32[1024,128]{1,0:T(8,128)S(1)} %copy-done.6, s32[512]{0:T(512)} %bitcast.91, bf16[512,128]{1,0:T(8,128)(2,1)S(1)} %bitcast.72), kind=kCustom, calls=%fused_computation.25 | custom fusion | flops 131072 | bytes 655360 | tf_op jit(solution)/shard_map/scatter-add | solution.py:102
  64.3 1.2 gather_fusion.4
  66.3 7.5 %scatter_custom_fusion.2 = f32[512,128]{1,0:T(8,128)} fusion(s32[1024]{0:T(1024)S(1)} %bitcast.90, bf16[1024,128]{1,0:T(8,128)(2,1)} %bitcast.31, f32[]{:T(128)} %constant.15.clone.1), kind=kCustom, calls=%fused_computation.18 | custom fusion | flops 262144 | bytes 524292 | tf_op jit(solution)/shard_map/scatter-add | solution.py:87
  74.2 3.4 %fusion.2 = f32[512,1024]{1,0:T(8,128)} fusion(bf16[32,8,4,128]{3,2,1,0:T(4,128)(2,1)} %bitcast.76, f32[256,1024]{1,0:T(8,128)} %copy-done.18, f32[1024]{0:T(1024)} %param.18, f32[256]{0:T(256)S(1)} %copy-done.15), kind=kOutput, calls=%fused_computation.20 | convolution fusion | flops 271056896 | bytes 3412992 | tf_op jit(solution)/shard_map/dot_general | solution.py:68
  78.8 1.2 gather_fusion.3
  80.1 1.2 gather_fusion.6
  82.0 1.5 scatter_fusion.2
  83.9 39.8 %psum.15 = f32[1024]{0:T(1024)} all-reduce(f32[1024]{0:T(1024)S(1)} %bitcast.81), channel_id=1, replica_groups=mesh['dp'=8,'rep'=4] {'dp','rep'}, use_global_device_ids=true, to_apply=%region_13.14 | all-reduce | flops 1024 | bytes 8192 | tf_op jit(solution)/shard_map/psum | solution.py:110
  123.7 68.5 %all-reduce.2.cloned.1.call-done = f32[3,128,128]{2,1,0:T(8,128)} async-done(((f32[3,128,128]{2,1,0:T(8,128)}), f32[3,128,128]{2,1,0:T(8,128)}) %all-reduce.2.cloned.1.call-update) | async-done | bytes 196624 | tf_op jit(solution)/shard_map/psum | solution.py:110
  192.1 1.3 multiply_add_fusion
  195.9 5.8 %all_gather.7 = f32[512,128]{1,0:T(8,128)S(1)} all-gather(f32[128,128]{1,0:T(8,128)S(1)} %get-tuple-element.9), channel_id=1, replica_groups=mesh['dp'=8,'rep'=4] {'rep'}, dimensions={0}, use_global_device_ids=true | all-gather | bytes 327680 | tf_op jit(solution)/shard_map/all_gather | solution.py:97
  201.7 5.8 %all_gather.6 = f32[512,128]{1,0:T(8,128)S(1)} all-gather(f32[128,128]{1,0:T(8,128)S(1)} %get-tuple-element.10), channel_id=1, replica_groups=mesh['dp'=8,'rep'=4] {'rep'}, dimensions={0}, use_global_device_ids=true | all-gather | bytes 327680 | tf_op jit(solution)/shard_map/all_gather | solution.py:96
  207.6 28.9 %reduce-scatter.5.cloned.1.call-done = f32[16,1024]{1,0:T(8,128)} async-done(((f32[512,1024]{1,0:T(8,128)}), f32[16,1024]{1,0:T(8,128)}) %reduce-scatter.5.cloned.1.call-update) | async-done | bytes 65552 | tf_op jit(solution)/shard_map/reduce_scatter | solution.py:67
  (81 shorter events, 16.5 us)
Async XLA Ops:
  8.0 36.4 %copy-start = (bf16[512,1024]{1,0:T(8,128)(2,1)S(1)}, bf16[512,1024]{1,0:T(8,128)(2,1)}, u32[]{:S(2)}) copy-start(bf16[512,1024]{1,0:T(8,128)(2,1)} %param.17) | copy-start | bytes 3145732
  8.0 1.4 copy-start.9
  8.0 19.1 %copy-start.2 = (f32[512,128]{1,0:T(8,128)S(1)}, f32[512,128]{1,0:T(8,128)}, u32[]{:S(2)}) copy-start(f32[512,128]{1,0:T(8,128)} %param.19) | copy-start | bytes 786436
  8.0 1.3 copy-start.7
  9.3 25.3 %copy-start.10 = (s32[256,2]{0,1:T(2,128)S(1)}, s32[256,2]{0,1:T(2,128)}, u32[]{:S(2)}) copy-start(s32[256,2]{0,1:T(2,128)} %param.13) | copy-start | bytes 6148
  27.1 8.9 %copy-start.17 = (s32[3]{0:T(128)S(1)}, s32[3]{0:T(128)}, u32[]{:S(2)}) copy-start(s32[3]{0:T(128)} %param.24) | copy-start | bytes 40
  31.2 11.6 %all-to-all-start.1 = ((bf16[8,128,128]{2,1,0:T(8,128)(2,1)}), bf16[8,128,128]{2,1,0:T(8,128)(2,1)S(1)}, u32[]{:S(2)}, u32[]{:S(2)}) async-start(bf16[8,128,128]{2,1,0:T(8,128)(2,1)} %bitcast.12), calls=%async_computation.1 | async-start | bytes 524288 | tf_op jit(solution)/shard_map/all_to_all | solution.py:51
  44.4 0.7 copy-start.8
  44.4 0.7 copy-start.13
  44.4 1.2 copy-start.16
  45.1 1.0 copy-start.18
  45.7 0.6 copy-start.14
  46.3 11.9 %copy-start.11 = (s32[3]{0:T(128)S(1)}, s32[3]{0:T(128)}, u32[]{:S(2)}) copy-start(s32[3]{0:T(128)} %compare_select_fusion.5) | copy-start | bytes 40
  47.6 13.0 %copy-start.6 = (f32[1024,128]{1,0:T(8,128)S(1)}, f32[1024,128]{1,0:T(8,128)}, u32[]{:S(2)}) copy-start(f32[1024,128]{1,0:T(8,128)} %param.23) | copy-start | bytes 1572868
  54.1 12.3 %all-to-all-start.2 = ((bf16[8,128,128]{2,1,0:T(8,128)(2,1)}), bf16[8,128,128]{2,1,0:T(8,128)(2,1)}, u32[]{:S(2)}, u32[]{:S(2)}) async-start(bf16[8,128,128]{2,1,0:T(8,128)(2,1)} %bitcast.71), calls=%async_computation.2 | async-start | bytes 524288 | tf_op jit(solution)/shard_map/all_to_all | solution.py:82
  58.1 134.0 %all-reduce.2.cloned.1.call-start = ((), (), s32[]{:S(2)}) async-start(), calls=%async_computation.6 | async-start | bytes 393216 | tf_op jit(solution)/shard_map/psum | solution.py:110
  59.0 15.2 %copy-start.15 = (f32[256]{0:T(256)S(1)}, f32[256]{0:T(256)}, u32[]{:S(2)}) copy-start(f32[256]{0:T(256)} %copy-done.14) | copy-start | bytes 3076
  65.5 129.3 %reduce-scatter.3.cloned.1.call-start = ((), (), s32[]{:S(2)}) async-start(), calls=%async_computation.5 | async-start | bytes 327680 | tf_op jit(solution)/shard_map/reduce_scatter | solution.py:91
  73.9 162.5 %reduce-scatter.5.cloned.1.call-start = ((), (), s32[]{:S(2)}) async-start(), calls=%async_computation.7 | async-start | bytes 2162688 | tf_op jit(solution)/shard_map/reduce_scatter | solution.py:67
  77.5 0.7 copy-start.1
  77.5 4.5 %copy-start.12 = (s32[3]{0:T(128)S(1)}, s32[3]{0:T(128)}, u32[]{:S(2)}) copy-start(s32[3]{0:T(128)} %compare_select_fusion.5) | copy-start | bytes 40
  83.6 153.6 %copy-start.5 = (f32[8,128,128]{2,1,0:T(8,128)}, f32[8,128,128]{2,1,0:T(8,128)S(1)}, u32[]{:S(2)}) copy-start(f32[8,128,128]{2,1,0:T(8,128)S(1)} %scatter_fusion.2) | copy-start | bytes 1572868
  194.1 43.7 %copy-start.4 = (f32[8,128,128]{2,1,0:T(8,128)}, f32[8,128,128]{2,1,0:T(8,128)S(1)}, u32[]{:S(2)}) copy-start(f32[8,128,128]{2,1,0:T(8,128)S(1)} %scatter_fusion.1) | copy-start | bytes 1572868
  194.8 43.1 %copy-start.3 = (f32[8,128,128]{2,1,0:T(8,128)}, f32[8,128,128]{2,1,0:T(8,128)S(1)}, u32[]{:S(2)}) copy-start(f32[8,128,128]{2,1,0:T(8,128)S(1)} %scatter_fusion) | copy-start | bytes 1572868
Sparse Core Ops, SparseCore 0:
  65.7 126.4 all-reduce.1
Sparse Core Ops, SparseCore 1:
  74.0 21.2 reduce-scatter.2
  97.9 138.4 reduce-scatter.4
where the time goes:
time: 246 us; the launch traced here: 245 us
  waiting for transfers between devices  104 us (42%)
  blocking collectives  65 us (26%)
  local copies, waits for them, and re-layouts  30 us (12%)
  other arithmetic  16.3 us (7%)
  between operations  15.8 us (6%)
  starting transfers between devices  7.76 us (3%)
  matrix products  6.01 us (2%)
    psum x1, waiting for transfers between devices, local(): picked_sum, out_grad = lax.psum((picked, head_term), ('dp', 'rep'))  68.5 us
    psum x1, blocking collectives, local(): picked_sum, out_grad = lax.psum((picked, head_term), ('dp', 'rep'))  39.8 us
    reduce_scatter x1, waiting for transfers between devices, local(): lax.psum_scatter(lax.dot_general(inputs, dhidden, (((0,), (0,)), ((), ())...  28.9 us
    all_to_all x1, blocking collectives, local(): lax.all_to_all(requests, 'dp', split_axis=0, concat_axis=0, tiled=True)  13.6 us
    scatter-add x1, other arithmetic, local(): cold_grad = jnp.zeros((own_rows, width), jnp.float32).at[asked.reshape(-1...  7.55 us
    all_to_all x1, waiting for transfers between devices, local(): lax.all_to_all(found, 'dp', split_axis=0, concat_axis=0, tiled=True)  6.23 us
    all_gather x1, blocking collectives, local(): lax.all_gather(table_updated, 'rep', axis=0, tiled=True)  5.84 us
    all_gather x1, blocking collectives, local(): lax.all_gather(accum_updated, 'rep', axis=0, tiled=True)  5.83 us
  transfers between devices with their start and end apart: 5, of which 4 were waited for; matrix products, arithmetic and copies ran while one was open for 12% of the time, Pallas kernels for 0%

commit v1 on v0

--- a/solution.py
+++ b/solution.py
@@ -1,9 +1,14 @@
+import functools
+
 import jax
 import jax.numpy as jnp
 from jax import lax
+from jax.experimental import pallas as pl
+from jax.experimental.pallas import tpu as pltpu
 from jax.sharding import PartitionSpec as P
 
 BLOCK = 128
+MESH = pl.DeviceIdType.MESH
 
 
 step_size = 0.5
@@ -13,6 +18,257 @@
 def adagrad(table_rows, accum_rows, gradient):
     accum_next = accum_rows + gradient * gradient
     return (table_rows - step_size * gradient / (jnp.sqrt(accum_next) + epsilon), accum_next)
+
+
+def bit_of(index, weight):
+    return lax.rem(lax.div(index, weight), 2)
+
+
+def flipped(index, weight):
+    return index + weight * (1 - 2 * bit_of(index, weight))
+
+
+def greet(devices):
+    barrier = pltpu.get_barrier_semaphore()
+    for device in devices:
+        pl.semaphore_signal(barrier, inc=1, device_id=device, device_id_type=MESH)
+    pl.semaphore_wait(barrier, len(devices))
+
+
+def chosen(offsets, rows):
+    shape = (rows, offsets.shape[1])
+    asks = lax.broadcasted_iota(jnp.int32, shape, 0) == jnp.broadcast_to(offsets, shape)
+    return jnp.where(asks, 1.0, 0.0).astype(jnp.bfloat16)
+
+
+def fetch_kernel(n, requests, table, asked_out, returned_out, asked, found, returned, sems):
+    me, rep = lax.axis_index("dp"), lax.axis_index("rep")
+    peers = [lax.rem(me + j, n) for j in range(1, n)]
+    sources = [lax.rem(me + n - j, n) for j in range(1, n)]
+    greet([(peer, rep) for peer in peers])
+    asking = []
+    for j, peer in enumerate(peers):
+        copy = pltpu.make_async_remote_copy(
+            requests.at[peer], asked.at[me], sems.at[0, j], sems.at[1, j], (peer, rep), MESH
+        )
+        copy.start()
+        asking.append(copy)
+    rows = table[...].astype(jnp.bfloat16)
+
+    def rows_of(offsets):
+        return lax.dot_general(
+            chosen(offsets, rows.shape[0]),
+            rows,
+            (((0,), (0,)), ((), ())),
+            preferred_element_type=jnp.float32,
+        ).astype(jnp.bfloat16)
+
+    asked[me] = requests[me]
+    returned[me] = rows_of(requests[me])
+    answers = []
+    for j, source in enumerate(sources):
+        asking[j].wait_recv()
+        found[j] = rows_of(asked[source])
+        copy = pltpu.make_async_remote_copy(
+            found.at[j], returned.at[me], sems.at[2, j], sems.at[3, j], (source, rep), MESH
+        )
+        copy.start()
+        answers.append(copy)
+    asked_out[...] = asked[...]
+    for j in range(n - 1):
+        asking[j].wait_send()
+        answers[j].wait()
+    returned_out[...] = returned[...]
+
+
+def fetch(requests, table):
+    n, cap = requests.shape
+    width = table.shape[1]
+    vmem = pl.BlockSpec(memory_space=pltpu.VMEM)
+    asked, returned = pl.pallas_call(
+        functools.partial(fetch_kernel, n),
+        out_shape=(
+            jax.ShapeDtypeStruct((n, 1, cap), jnp.int32),
+            jax.ShapeDtypeStruct((n, cap, width), jnp.bfloat16),
+        ),
+        in_specs=[vmem] * 2,
+        out_specs=(vmem, vmem),
+        scratch_shapes=[
+            pltpu.VMEM((n, 1, cap), jnp.int32),
+            pltpu.VMEM((n - 1, cap, width), jnp.bfloat16),
+            pltpu.VMEM((n, cap, width), jnp.bfloat16),
+            pltpu.SemaphoreType.DMA((4, n - 1)),
+        ],
+        compiler_params=pltpu.CompilerParams(collective_id=0, has_side_effects=True),
+    )(requests.reshape(n, 1, cap), table)
+    return asked, returned
+
+
+def combine_kernel(
+    n, links, top, hot, outgoing, asked, table, accum,
+    top_out, hot_out, table_out, accum_out,
+    incoming, cold, cold_half, cold_got, cold_last, table_all, accum_all,
+    top_got, a_parts, a_gots, b_parts, b_gots, h_parts, h_gots, h_news, sends, recvs,
+):
+    me, rep = lax.axis_index("dp"), lax.axis_index("rep")
+    core, side = bit_of(rep, 1), bit_of(rep, 2)
+    over_core, over_side = (me, flipped(rep, 1)), (me, flipped(rep, 2))
+    weights = [1 << k for k in range(links)]
+    dp_bits = [bit_of(me, weight) for weight in weights]
+    over_dp = [(flipped(me, weight), rep) for weight in weights]
+    peers = [lax.rem(me + j, n) for j in range(1, n)]
+    sources = [lax.rem(me + n - j, n) for j in range(1, n)]
+    greet([(peer, rep) for peer in peers] + [over_core, over_side])
+    count = [0]
+
+    def send(src, dst, device):
+        k = count[0]
+        count[0] += 1
+        copy = pltpu.make_async_remote_copy(src, dst, sends.at[k], recvs.at[k], device, MESH)
+        copy.start()
+        return copy
+
+    top_copy = send(top.at[:, 1 - core], top_got, over_core)
+    cold_copies = [
+        send(outgoing.at[peer], incoming.at[me], (peer, rep)) for peer in peers
+    ]
+    hot_copy = send(hot.at[:, 1 - core], h_gots[0], over_core)
+
+    a_route = [(side, over_side)] + list(zip(dp_bits, over_dp))
+    b_route = [(dp_bits[0], over_dp[0]), (side, over_side)] + list(zip(dp_bits, over_dp))[1:]
+    h_route = [(core, over_core)] + a_route
+
+    def step_on(parts, gots, route, k, copy):
+        bit = route[k][0]
+        copy.wait()
+        kept = parts[k][:, bit] + gots[k][...]
+        if k + 1 == len(route):
+            return kept
+        parts[k + 1][...] = kept.reshape(parts[k + 1].shape)
+        next_bit, device = route[k + 1]
+        return send(parts[k + 1].at[:, 1 - next_bit], gots[k + 1], device)
+
+    top_copy.wait()
+    half = top.shape[3] // 2
+    a_parts[0][...] = (top[:, core, :, :half] + top_got[:, :, :half]).reshape(a_parts[0].shape)
+    a_copy = send(a_parts[0].at[:, 1 - side], a_gots[0], over_side)
+    b_parts[0][...] = (top[:, core, :, half:] + top_got[:, :, half:]).reshape(b_parts[0].shape)
+    b_copy = send(b_parts[0].at[:, 1 - dp_bits[0]], b_gots[0], over_dp[0])
+    all_h = [hot] + list(h_parts)
+    hot_copy = step_on(all_h, h_gots, h_route, 0, hot_copy)
+
+    own_rows = 4 * table.shape[0]
+    total = jnp.dot(
+        chosen(asked[me], own_rows), outgoing[me], preferred_element_type=jnp.float32
+    )
+    for j, source in enumerate(sources):
+        cold_copies[j].wait_recv()
+        total += jnp.dot(
+            chosen(asked[source], own_rows), incoming[source], preferred_element_type=jnp.float32
+        )
+    cold[...] = total.reshape(cold.shape)
+    cold_copy = send(cold.at[:, 1 - core], cold_got, over_core)
+    hot_copy = step_on(all_h, h_gots, h_route, 1, hot_copy)
+    cold_copy.wait()
+    cold_half[...] = cold[:, core] + cold_got[...]
+    cold_copy = send(cold_half.at[1 - side], cold_last, over_side)
+    a_copy = step_on(a_parts, a_gots, a_route, 0, a_copy)
+    b_copy = step_on(b_parts, b_gots, b_route, 0, b_copy)
+    hot_copy = step_on(all_h, h_gots, h_route, 2, hot_copy)
+    cold_copy.wait()
+    table_next, accum_next = adagrad(table[...], accum[...], cold_half[side] + cold_last[...])
+    table_all[side, core] = table_next
+    accum_all[side, core] = accum_next
+    pair = [send(ref.at[side, core], ref.at[side, core], over_side) for ref in (table_all, accum_all)]
+    last = len(a_route)
+    for k in range(1, last):
+        if k + 2 <= last:
+            hot_copy = step_on(all_h, h_gots, h_route, k + 2, hot_copy)
+        if k + 2 == last:
+            cur = h_news[0]
+            cur[...] = hot_copy
+            bit, device = h_route[-1]
+            hot_step = send(cur, h_news[1].at[:, bit], device)
+            h_news[1][:, bit] = cur[...]
+        a_copy = step_on(a_parts, a_gots, a_route, k, a_copy)
+        b_copy = step_on(b_parts, b_gots, b_route, k, b_copy)
+        if k == 1:
+            for copy in pair:
+                copy.wait()
+            pair = [send(ref.at[:, core], ref.at[:, core], over_core) for ref in (table_all, accum_all)]
+    top_out[:, :half] = a_copy.reshape(top_out.shape[0], half)
+    top_out[:, half:] = b_copy.reshape(top_out.shape[0], half)
+    for copy in pair:
+        copy.wait()
+    table_out[...] = table_all[...]
+    accum_out[...] = accum_all[...]
+    for k in range(len(h_route) - 2, -1, -1):
+        hot_step.wait()
+        stage = 2 * (len(h_route) - 2 - k)
+        got, cur, new = h_news[stage + 1], h_news[stage + 2], h_news[stage + 3]
+        cur[...] = got[...].reshape(cur.shape)
+        bit, device = h_route[k]
+        hot_step = send(cur, new.at[:, bit], device)
+        new[:, bit] = cur[...]
+    hot_step.wait()
+    hot_out[...] = h_news[-1][...]
+    for copy in cold_copies:
+        copy.wait_send()
+
+
+def combine(top, hot, outgoing, asked, table, accum):
+    n, cap, width = outgoing.shape
+    devices = 4 * n
+    links = n.bit_length() - 1
+    rows, columns = top.shape[0] // devices, top.shape[1]
+    hot_rows = hot.shape[0] // devices
+    quarter = table.shape[0]
+    half = columns // 2
+    f32 = lambda *shape: pltpu.VMEM(shape, jnp.float32)
+    steps = [2**k for k in range(links, -1, -1)]
+    a_parts = [f32(m, 2, rows, half) for m in steps]
+    a_gots = [f32(m, rows, half) for m in steps]
+    b_parts = [f32(n // 2, 2, 2, rows, half), f32(n // 2, 2, rows, half)] + a_parts[2:]
+    b_gots = [f32(n // 2, 2, rows, half), f32(n // 2, rows, half)] + a_gots[2:]
+    h_parts = [f32(m, 2, hot_rows, width) for m in steps]
+    h_gots = [f32(m, hot_rows, width) for m in [2 * n] + steps]
+    h_news = []
+    for m in steps[::-1] + [2 * n]:
+        h_news += [f32(m, hot_rows, width), f32(m, 2, hot_rows, width)]
+    copies = 1 + (n - 1) + 2 * (links + 1) + 2 * (links + 2) + 2 + 4
+    vmem = pl.BlockSpec(memory_space=pltpu.VMEM)
+    out = lambda *shape: jax.ShapeDtypeStruct(shape, jnp.float32)
+    square = (2, 2, quarter, width)
+    return pl.pallas_call(
+        functools.partial(combine_kernel, n, links),
+        out_shape=(
+            out(rows, columns), out(2 * n, 2, hot_rows, width), out(*square), out(*square)
+        ),
+        in_specs=[vmem] * 6,
+        out_specs=(vmem,) * 4,
+        scratch_shapes=[
+            pltpu.VMEM((n, cap, width), jnp.bfloat16),
+            f32(*square),
+            f32(2, quarter, width),
+            f32(2, quarter, width),
+            f32(quarter, width),
+            f32(*square),
+            f32(*square),
+            f32(2 * n, rows, columns),
+            a_parts, a_gots, b_parts, b_gots, h_parts, h_gots, h_news,
+            pltpu.SemaphoreType.DMA((copies,)),
+            pltpu.SemaphoreType.DMA((copies,)),
+        ],
+        compiler_params=pltpu.CompilerParams(collective_id=1, has_side_effects=True),
+    )(
+        top.reshape(2 * n, 2, rows, columns),
+        hot.reshape(2 * n, 2, hot_rows, width),
+        outgoing, asked, table, accum,
+    )
+
+
+def suits(n, rep_n, top_rows):
+    return rep_n == 4 and n >= 2 and n & (n - 1) == 0 and top_rows % (8 * n * rep_n) == 0
 
 
 def local(
@@ -46,9 +302,13 @@
     targets = owners * capacity + positions
     requests = jnp.zeros((owners_count * capacity,), jnp.int32).at[targets].set(cold_offset)
     requests = requests.reshape(owners_count, capacity)
-    asked = lax.all_to_all(requests, "dp", split_axis=0, concat_axis=0, tiled=True)
-    found = cold_table[asked].astype(jnp.bfloat16)
-    returned = lax.all_to_all(found, "dp", split_axis=0, concat_axis=0, tiled=True)
+    direct = suits(owners_count, lax.axis_size("rep"), top_weight.shape[0])
+    if direct:
+        asked, returned = fetch(requests, cold_table)
+    else:
+        asked = lax.all_to_all(requests, "dp", split_axis=0, concat_axis=0, tiled=True)
+        found = cold_table[asked].astype(jnp.bfloat16)
+        returned = lax.all_to_all(found, "dp", split_axis=0, concat_axis=0, tiled=True)
     cold_rows = returned.reshape(owners_count * capacity, width)[targets]
     cold_rows = cold_rows.reshape(samples, cold_feats, width)
     hot_rows = hot_cache[hot_ids].astype(jnp.bfloat16)
@@ -64,13 +324,8 @@
     slope = gates * (1.0 + preact * (1.0 - gates))
     dhidden = (errors[:, None] * out_weight[None, :] * slope).astype(jnp.bfloat16)
     head_term = jnp.dot(errors, hidden_wide, precision=lax.Precision.HIGHEST)
-    top_grad = lax.psum_scatter(
-        lax.dot_general(
-            inputs, dhidden, (((0,), (0,)), ((), ())), preferred_element_type=jnp.float32
-        ),
-        ("dp", "rep"),
-        scatter_dimension=0,
-        tiled=True,
+    top_part = lax.dot_general(
+        inputs, dhidden, (((0,), (0,)), ((), ())), preferred_element_type=jnp.float32
     )
     dinputs = lax.dot_general(
         dhidden, top_weight, (((1,), (1,)), ((), ())), preferred_element_type=jnp.float32
@@ -79,27 +334,18 @@
     cold_dx = dinputs[:, hot_feats:].reshape(lookups, width)
     outgoing = jnp.zeros((owners_count * capacity, width), jnp.bfloat16).at[targets].set(cold_dx)
     outgoing = outgoing.reshape(owners_count, capacity, width)
-    incoming = lax.all_to_all(outgoing, "dp", split_axis=0, concat_axis=0, tiled=True)
     own_rows = cold_table.shape[0]
-    cold_grad = (
-        jnp.zeros((own_rows, width), jnp.float32)
-        .at[asked.reshape(-1)]
-        .add(incoming.reshape(-1, width).astype(jnp.float32))
-    )
     quarter = own_rows // lax.axis_size("rep")
     offset_rows = lax.axis_index("rep") * quarter
-    cold_share = lax.psum_scatter(cold_grad, "rep", scatter_dimension=0, tiled=True)
     table_share = lax.dynamic_slice_in_dim(cold_table, offset_rows, quarter, 0)
     accum_share = lax.dynamic_slice_in_dim(cold_accum, offset_rows, quarter, 0)
-    table_updated, accum_updated = adagrad(table_share, accum_share, cold_share)
-    cold_table_new, cold_accum_new = (
-        lax.all_gather(table_updated, "rep", axis=0, tiled=True),
-        lax.all_gather(accum_updated, "rep", axis=0, tiled=True),
-    )
     hot_count = hot_cache.shape[0]
     blocks_count = hot_count // BLOCK
-    hot_dx = dinputs[:, :hot_feats].reshape(samples * hot_feats, width).astype(jnp.float32)
-    hot_grad = jnp.zeros((hot_count, width), jnp.float32).at[hot_ids.reshape(-1)].add(hot_dx)
+    hot_dx = dinputs[:, :hot_feats].reshape(samples * hot_feats, width)
+    hot_named = (
+        jnp.arange(hot_count, dtype=jnp.int32)[:, None] == hot_ids.reshape(-1)[None, :]
+    ).astype(jnp.bfloat16)
+    hot_grad = jnp.dot(hot_named, hot_dx, preferred_element_type=jnp.float32)
     carried = (pending + hot_grad).reshape(blocks_count, BLOCK, width)
     picked = carried[refresh_blocks]
     divisors = 1.0 + block_clock[refresh_blocks].astype(jnp.float32)
@@ -107,7 +353,41 @@
     accum_blocks = hot_accum.reshape(blocks_count, BLOCK, width)
     cache_chosen = cache_blocks[refresh_blocks]
     accum_chosen = accum_blocks[refresh_blocks]
-    picked_sum, out_grad = lax.psum((picked, head_term), ("dp", "rep"))
+    if direct:
+        picked_rows = refresh_blocks.shape[0] * BLOCK
+        head_rows = head_term.shape[0] // width
+        even = 8 * owners_count * lax.axis_size("rep")
+        spare = -(picked_rows + head_rows) % even
+        summands = jnp.concatenate(
+            [
+                picked.reshape(picked_rows, width),
+                head_term.reshape(head_rows, width),
+                jnp.zeros((spare, width), jnp.float32),
+            ]
+        )
+        top_grad, sums, cold_table_new, cold_accum_new = combine(
+            top_part, summands, outgoing, asked, table_share, accum_share
+        )
+        cold_table_new = cold_table_new.reshape(own_rows, width)
+        cold_accum_new = cold_accum_new.reshape(own_rows, width)
+        sums = sums.reshape(-1, width)
+        picked_sum = sums[:picked_rows].reshape(picked.shape)
+        out_grad = sums[picked_rows : picked_rows + head_rows].reshape(-1)
+    else:
+        incoming = lax.all_to_all(outgoing, "dp", split_axis=0, concat_axis=0, tiled=True)
+        cold_grad = (
+            jnp.zeros((own_rows, width), jnp.float32)
+            .at[asked.reshape(-1)]
+            .add(incoming.reshape(-1, width).astype(jnp.float32))
+        )
+        cold_share = lax.psum_scatter(cold_grad, "rep", scatter_dimension=0, tiled=True)
+        table_updated, accum_updated = adagrad(table_share, accum_share, cold_share)
+        cold_table_new, cold_accum_new = (
+            lax.all_gather(table_updated, "rep", axis=0, tiled=True),
+            lax.all_gather(accum_updated, "rep", axis=0, tiled=True),
+        )
+        top_grad = lax.psum_scatter(top_part, ("dp", "rep"), scatter_dimension=0, tiled=True)
+        picked_sum, out_grad = lax.psum((picked, head_term), ("dp", "rep"))
     flush = picked_sum / divisors[:, None, None]
     cache_part, accum_part = adagrad(cache_chosen, accum_chosen, flush)
     hot_cache_new = cache_blocks.at[refresh_blocks].set(cache_part).reshape(hot_count, width)

time: 246 us -> 92.6 us (0.38)
  waiting for transfers between devices: 104 us -> 0 us
  blocking collectives: 65 us -> 0 us
  Pallas kernels: 0 us -> 58 us
  between operations: 15.8 us -> 0.99 us
  other arithmetic: 16.3 us -> 3.31 us
  starting transfers between devices: 7.76 us -> 0 us
  local copies, waits for them, and re-layouts: 30 us -> 25.2 us
    psum x1 -> x0, waiting for transfers between devices: 68.5 us -> none  [local(): picked_sum, out_grad = lax.psum((picked, head_term), ('dp', 'rep'))]
    pallas_call x0 -> x2, Pallas kernels: none -> 58 us  [the longest x1 40.6 us: combine(): pl.pallas_call(functools.partial(combine_kernel, n, links), out_shape=(ou...]
    psum x1 -> x0, blocking collectives: 39.8 us -> none  [local(): picked_sum, out_grad = lax.psum((picked, head_term), ('dp', 'rep'))]
    reduce_scatter x2 -> x0, waiting for transfers between devices: 28.9 us -> none  [the longest x1 28.9 us: local(): lax.psum_scatter(lax.dot_general(inputs, dhidden, (((0,), (0,)), ((), ())...]
    all_to_all x1 -> x0, blocking collectives: 13.6 us -> none  [local(): lax.all_to_all(requests, 'dp', split_axis=0, concat_axis=0, tiled=True)]
    all_gather x2 -> x0, blocking collectives: 11.7 us -> none  [the longest x1 5.84 us: local(): lax.all_gather(table_updated, 'rep', axis=0, tiled=True)]
    scatter-add x2 -> x0, other arithmetic: 11.2 us -> none  [the longest x1 7.55 us: local(): cold_grad = jnp.zeros((own_rows, width), jnp.float32).at[asked.reshape(-1...]
    all_to_all x2 -> x0, starting transfers between devices: 7.45 us -> none  [the longest x1 4.04 us: local(): lax.all_to_all(outgoing, 'dp', split_axis=0, concat_axis=0, tiled=True)]
  transfers between devices with their start and end apart: 5 -> 0, of which waited for: 4 -> 0; matrix products, arithmetic and copies ran while one was open for 12% -> 0% of each run, Pallas kernels for 0% -> 0%
where the time goes in v1:
time: 92.6 us; the launch traced here: 92.1 us
  Pallas kernels  58 us (63%)
  local copies, waits for them, and re-layouts  25.2 us (27%)
  matrix products  4.57 us (5%)
  other arithmetic  3.31 us (4%)
  between operations  0.99 us (1%)
    pallas_call x1, Pallas kernels, combine(): pl.pallas_call(functools.partial(combine_kernel, n, links), out_shape=(ou...  40.6 us
    pallas_call x1, Pallas kernels, fetch(): pl.pallas_call(functools.partial(fetch_kernel, n), out_shape=(jax.ShapeDt...  17.4 us
    unnamed x30, local copies, waits for them, and re-layouts  6.4 us
    scatter x1, local copies, waits for them, and re-layouts, local(): jnp.zeros((owners_count * capacity,), jnp.int32).at[targets]  3.17 us
    scatter x1, local copies, waits for them, and re-layouts, local(): jnp.zeros((owners_count * capacity, width), jnp.bfloat16).at[targets]  2.43 us
    dot_general x1, matrix products, local(): lax.dot_general(inputs, dhidden, (((0,), (0,)), ((), ())), preferred_elem...  2.09 us
    gather x1, local copies, waits for them, and re-layouts, local(): cold_rows = returned.reshape(owners_count * capacity, width)[targets]  2.04 us

profile of v1, /device:TPU:0, one launch (start us, length us, event | category | flops | bytes accessed | tf_op | source)
XLA Modules:
  0.0 92.1 jit_solution(16012542890831886035)
XLA Ops:
  0.7 1.1 %copy.33 = f32[1024,128]{1,0:T(8,128)S(1)} copy(f32[1024,128]{1,0:T(8,128)} %param.21) | data formatting | bytes 1048576
  1.8 1.0 %copy.34 = f32[1024,128]{1,0:T(8,128)S(1)} copy(f32[1024,128]{1,0:T(8,128)} %param.22) | data formatting | bytes 1048576
  2.9 1.1 %reduce-window.6 = s32[8,4,128]{2,0,1:T(8,128)S(1)} reduce-window(s32[8,4,128]{2,0,1:T(8,128)S(1)} %fusion.9, s32[]{:T(128)} %constant.11.clone.1), window={size=1x1x128 pad=0_0x0_0x127_0}, to_apply=%region_0.0 | reduce-window | flops 520192 | bytes 32772 | tf_op jit(solution)/shard_map/reduce-window
  4.4 3.2 %scatter_custom_fusion = s32[1024]{0:T(1024)} fusion(s32[512]{0:T(512)S(1)} %bitcast.85, s32[512]{0:T(512)} %param.15, s32[]{:T(128)} %constant.11.clone.1), kind=kCustom, calls=%fused_computation.42 | custom fusion | bytes 4608 | tf_op jit(solution)/shard_map/scatter | solution.py:303
  7.5 17.4 %shard_map.180 = (s32[8,1,128]{2,1,0:T(1,128)}, bf16[8,128,128]{2,1,0:T(8,128)(2,1)}) custom-call(s32[8,1,128]{2,1,0:T(1,128)} %bitcast.84, f32[512,128]{1,0:T(8,128)} %table.1), custom_call_target="tpu_custom_call" | custom-call | tf_op jit(solution)/shard_map/pallas_call | solution.py:88
  25.0 2.0 %gather_fusion.1 = bf16[512,128]{1,0:T(8,128)(2,1)S(1)} fusion(bf16[1024,128]{1,0:T(8,128)(2,1)} %bitcast.61, s32[1024]{0:T(1024)S(1)} %pad_clamp_fusion.1), kind=kCustom, calls=%fused_computation.1 | custom fusion | bytes 264192 | tf_op jit(solution)/shard_map/gather | solution.py:312
  27.4 1.1 %gather_fusion = bf16[512,128]{1,0:T(8,128)(2,1)S(1)} fusion(f32[1024,128]{1,0:T(8,128)S(1)} %copy.33, s32[1024]{0:T(1024)S(1)} %pad_clamp_fusion.2), kind=kCustom, calls=%fused_computation | custom fusion | bytes 264192 | tf_op jit(solution)/shard_map/gather | solution.py:314
  28.9 0.6 multiply_convert_fusion.1
  30.1 2.1 %fusion.3.top = f32[16,2,16,1024]{3,2,1,0:T(8,128)} fusion(bf16[16,2,16,256]{3,2,1,0:T(8,128)(2,1)S(1)} %bitcast.78, f32[256,1024]{1,0:T(8,128)S(1)} %get-tuple-element.24, f32[1024]{0:T(1024)S(1)} %copy-done.9, f32[256]{0:T(256)S(1)} %divide_subtract_fusion.1), kind=kOutput, calls=%fused_computation.19 | convolution fusion | flops 271056896 | bytes 3412992 | tf_op jit(solution)/shard_map/dot_general | solution.py:327
  32.5 0.6 convolution_convert_fusion
  34.9 0.8 maximum_maximum_fusion
  35.7 2.4 %scatter_custom_fusion.1 = bf16[1024,128]{1,0:T(8,128)(2,1)} fusion(s32[512]{0:T(512)S(1)} %bitcast.87, bf16[512,128]{1,0:T(8,128)(2,1)S(1)} %bitcast.80, bf16[]{:T(256)} %constant.17.clone.1), kind=kCustom, calls=%fused_computation.25 | custom fusion | bytes 262146 | tf_op jit(solution)/shard_map/scatter | solution.py:335
  38.2 1.5 %constant_dynamic-slice_fusion = (f32[128,128]{1,0:T(8,128)}, f32[128,128]{1,0:T(8,128)}) fusion(f32[512,128]{1,0:T(8,128)} %param.20, s32[]{:T(128)S(6)} %select_n.12, f32[512,128]{1,0:T(8,128)} %table.1), kind=kLoop, calls=%fused_computation.46 | loop fusion | bytes 262148 | tf_op jit(solution)/shard_map/dynamic_slice | solution.py:341
  39.7 40.6 %shard_map.181 = (f32[16,1024]{1,0:T(8,128)}, f32[16,2,16,128]{3,2,1,0:T(8,128)}, f32[2,2,128,128]{3,2,1,0:T(8,128)}, f32[2,2,128,128]{3,2,1,0:T(8,128)}) custom-call(f32[16,2,16,1024]{3,2,1,0:T(8,128)} %fusion.3.top, f32[16,2,16,128]{3,2,1,0:T(8,128)} %bitcast.68, bf16[8,128,128]{2,1,0:T(8,128)(2,1)} %bitcast.69, s32[8,1,128]{2,1,0:T(1,128)} %get-tuple-element.14.asked, ...), custom_call_target="tpu_custom_call" | custom-call | tf_op jit(solution)/shard_map/pallas_call | solution.py:242
  80.9 0.9 %slice.23 = f32[12,2,16,128]{3,2,1,0:T(8,128)S(1)} slice(f32[16,2,16,128]{3,2,1,0:T(8,128)} %get-tuple-element.17), slice={[0:12], [0:2], [0:16], [0:128]} | slice | bytes 393216 | tf_op jit(solution)/shard_map/slice | solution.py:374
  81.8 0.6 gather_fusion.4
  83.0 0.9 multiply_add_fusion
  83.9 1.5 %scatter_fusion = f32[8,128,128]{2,1,0:T(8,128)S(1)} fusion(f32[8,128,128]{2,1,0:T(8,128)S(1)} %bitcast.59, s32[3]{0:T(128)S(1)} %compare_select_fusion.2, f32[3,128,128]{2,1,0:T(8,128)} %get-tuple-element.20), kind=kCustom, calls=%fused_computation.8 | custom fusion | bytes 589836 | tf_op jit(solution)/shard_map/scatter | solution.py:393
  85.5 0.7 scatter_fusion.1
  86.2 0.7 scatter_fusion.2
  86.8 1.3 %slice_bitcast_fusion = f32[1024]{0:T(1024)} fusion(f32[512,128]{1,0:T(8,128)} %bitcast.79), kind=kLoop, calls=%fused_computation.37 | loop fusion | bytes 8192 | tf_op jit(solution)/shard_map/reshape | solution.py:375
  88.1 1.7 %copy.35 = f32[512,128]{1,0:T(8,128)} copy(f32[512,128]{1,0:T(8,128)} %bitcast.76) | data formatting | bytes 524288
  89.8 1.7 %copy.36 = f32[512,128]{1,0:T(8,128)} copy(f32[512,128]{1,0:T(8,128)} %bitcast.75) | data formatting | bytes 524288
  91.4 0.6 copy.37
  (54 shorter events, 4.8 us)
Async XLA Ops:
  0.6 28.3 %copy-start = (bf16[512,1024]{1,0:T(8,128)(2,1)S(1)}, bf16[512,1024]{1,0:T(8,128)(2,1)}, u32[]{:S(2)}) copy-start(bf16[512,1024]{1,0:T(8,128)(2,1)} %param.17) | copy-start | bytes 3145732
  0.6 26.4 %copy-start.8 = (s32[256,2]{0,1:T(2,128)S(1)}, s32[256,2]{0,1:T(2,128)}, u32[]{:S(2)}) copy-start(s32[256,2]{0,1:T(2,128)} %param.13) | copy-start | bytes 6148
  0.7 2.2 %copy-start.7 = (s32[512,1]{0,1:T(1,128)S(1)}, s32[512,1]{0,1:T(1,128)}, u32[]{:S(2)}) copy-start(s32[512,1]{0,1:T(1,128)} %param.14) | copy-start | bytes 6148
  28.9 0.7 copy-start.9
  28.9 1.2 %copy-start.10 = (s32[256]{0:T(256)S(1)}, s32[256]{0:T(256)}, u32[]{:S(2)}) copy-start(s32[256]{0:T(256)} %param.16) | copy-start | bytes 3076
  32.5 1.2 %copy-start.5 = (f32[1024,128]{1,0:T(8,128)S(1)}, f32[1024,128]{1,0:T(8,128)}, u32[]{:S(2)}) copy-start(f32[1024,128]{1,0:T(8,128)} %param.23) | copy-start | bytes 1572868
  33.2 1.0 %copy-start.11 = (s32[3]{0:T(128)S(1)}, s32[3]{0:T(128)}, u32[]{:S(2)}) copy-start(s32[3]{0:T(128)} %param.24) | copy-start | bytes 40
  35.7 46.1 %copy-start.1 = (s32[8]{0:T(128)S(1)}, s32[8]{0:T(128)}, u32[]{:S(2)}) copy-start(s32[8]{0:T(128)} %param.25) | copy-start | bytes 100
  83.0 8.4 %copy-start.6 = (f32[16,1024]{1,0:T(8,128)S(1)}, f32[16,1024]{1,0:T(8,128)}, u32[]{:S(2)}) copy-start(f32[16,1024]{1,0:T(8,128)} %get-tuple-element.39) | copy-start | bytes 196612
  85.4 6.6 %copy-start.2 = (f32[8,128,128]{2,1,0:T(8,128)}, f32[8,128,128]{2,1,0:T(8,128)S(1)}, u32[]{:S(2)}) copy-start(f32[8,128,128]{2,1,0:T(8,128)S(1)} %scatter_fusion) | copy-start | bytes 1572868
  86.1 6.0 %copy-start.3 = (f32[8,128,128]{2,1,0:T(8,128)}, f32[8,128,128]{2,1,0:T(8,128)S(1)}, u32[]{:S(2)}) copy-start(f32[8,128,128]{2,1,0:T(8,128)S(1)} %scatter_fusion.1) | copy-start | bytes 1572868
  86.8 5.3 %copy-start.4 = (f32[8,128,128]{2,1,0:T(8,128)}, f32[8,128,128]{2,1,0:T(8,128)S(1)}, u32[]{:S(2)}) copy-start(f32[8,128,128]{2,1,0:T(8,128)S(1)} %scatter_fusion.2) | copy-start | bytes 1572868

commit v2 on v1

--- a/solution.py
+++ b/solution.py
@@ -128,11 +128,11 @@
         copy.start()
         return copy
 
+    hot_copy = send(hot.at[:, 1 - core], h_gots[0], over_core)
     top_copy = send(top.at[:, 1 - core], top_got, over_core)
     cold_copies = [
         send(outgoing.at[peer], incoming.at[me], (peer, rep)) for peer in peers
     ]
-    hot_copy = send(hot.at[:, 1 - core], h_gots[0], over_core)
 
     a_route = [(side, over_side)] + list(zip(dp_bits, over_dp))
     b_route = [(dp_bits[0], over_dp[0]), (side, over_side)] + list(zip(dp_bits, over_dp))[1:]
@@ -148,16 +148,43 @@
         next_bit, device = route[k + 1]
         return send(parts[k + 1].at[:, 1 - next_bit], gots[k + 1], device)
 
+    all_h = [hot] + list(h_parts)
+    hot_state = [0, hot_copy]
+
+    def spread(i):
+        bit, device = h_route[len(h_route) - 1 - i]
+        cur, new = h_news[2 * i], h_news[2 * i + 1]
+        hot_state[1] = send(cur, new.at[:, bit], device)
+        new[:, bit] = cur[...]
+
+    def advance_hot():
+        k, copy = hot_state
+        i = k - len(h_route)
+        hot_state[0] = k + 1
+        if i >= 0:
+            copy.wait()
+            if i + 1 < len(h_route):
+                cur = h_news[2 * i + 2]
+                cur[...] = h_news[2 * i + 1][...].reshape(cur.shape)
+                spread(i + 1)
+        else:
+            result = step_on(all_h, h_gots, h_route, k, copy)
+            if i == -1:
+                h_news[0][...] = result
+                spread(0)
+            else:
+                hot_state[1] = result
+
+    advance_hot()
     top_copy.wait()
     half = top.shape[3] // 2
     a_parts[0][...] = (top[:, core, :, :half] + top_got[:, :, :half]).reshape(a_parts[0].shape)
     a_copy = send(a_parts[0].at[:, 1 - side], a_gots[0], over_side)
     b_parts[0][...] = (top[:, core, :, half:] + top_got[:, :, half:]).reshape(b_parts[0].shape)
     b_copy = send(b_parts[0].at[:, 1 - dp_bits[0]], b_gots[0], over_dp[0])
-    all_h = [hot] + list(h_parts)
-    hot_copy = step_on(all_h, h_gots, h_route, 0, hot_copy)
-
-    own_rows = 4 * table.shape[0]
+    advance_hot()
+
+    own_rows = table.shape[0] * table.shape[1]
     total = jnp.dot(
         chosen(asked[me], own_rows), outgoing[me], preferred_element_type=jnp.float32
     )
@@ -168,49 +195,38 @@
         )
     cold[...] = total.reshape(cold.shape)
     cold_copy = send(cold.at[:, 1 - core], cold_got, over_core)
-    hot_copy = step_on(all_h, h_gots, h_route, 1, hot_copy)
+    advance_hot()
     cold_copy.wait()
     cold_half[...] = cold[:, core] + cold_got[...]
     cold_copy = send(cold_half.at[1 - side], cold_last, over_side)
+    advance_hot()
     a_copy = step_on(a_parts, a_gots, a_route, 0, a_copy)
     b_copy = step_on(b_parts, b_gots, b_route, 0, b_copy)
-    hot_copy = step_on(all_h, h_gots, h_route, 2, hot_copy)
+    advance_hot()
     cold_copy.wait()
-    table_next, accum_next = adagrad(table[...], accum[...], cold_half[side] + cold_last[...])
+    table_next, accum_next = adagrad(table[rep], accum[rep], cold_half[side] + cold_last[...])
     table_all[side, core] = table_next
     accum_all[side, core] = accum_next
     pair = [send(ref.at[side, core], ref.at[side, core], over_side) for ref in (table_all, accum_all)]
+    advance_hot()
     last = len(a_route)
     for k in range(1, last):
-        if k + 2 <= last:
-            hot_copy = step_on(all_h, h_gots, h_route, k + 2, hot_copy)
-        if k + 2 == last:
-            cur = h_news[0]
-            cur[...] = hot_copy
-            bit, device = h_route[-1]
-            hot_step = send(cur, h_news[1].at[:, bit], device)
-            h_news[1][:, bit] = cur[...]
         a_copy = step_on(a_parts, a_gots, a_route, k, a_copy)
         b_copy = step_on(b_parts, b_gots, b_route, k, b_copy)
         if k == 1:
             for copy in pair:
                 copy.wait()
             pair = [send(ref.at[:, core], ref.at[:, core], over_core) for ref in (table_all, accum_all)]
+        if hot_state[0] < 2 * len(h_route):
+            advance_hot()
     top_out[:, :half] = a_copy.reshape(top_out.shape[0], half)
     top_out[:, half:] = b_copy.reshape(top_out.shape[0], half)
     for copy in pair:
         copy.wait()
     table_out[...] = table_all[...]
     accum_out[...] = accum_all[...]
-    for k in range(len(h_route) - 2, -1, -1):
-        hot_step.wait()
-        stage = 2 * (len(h_route) - 2 - k)
-        got, cur, new = h_news[stage + 1], h_news[stage + 2], h_news[stage + 3]
-        cur[...] = got[...].reshape(cur.shape)
-        bit, device = h_route[k]
-        hot_step = send(cur, new.at[:, bit], device)
-        new[:, bit] = cur[...]
-    hot_step.wait()
+    while hot_state[0] < 2 * len(h_route):
+        advance_hot()
     hot_out[...] = h_news[-1][...]
     for copy in cold_copies:
         copy.wait_send()
@@ -222,7 +238,7 @@
     links = n.bit_length() - 1
     rows, columns = top.shape[0] // devices, top.shape[1]
     hot_rows = hot.shape[0] // devices
-    quarter = table.shape[0]
+    quarter = table.shape[0] // 4
     half = columns // 2
     f32 = lambda *shape: pltpu.VMEM(shape, jnp.float32)
     steps = [2**k for k in range(links, -1, -1)]
@@ -263,7 +279,9 @@
     )(
         top.reshape(2 * n, 2, rows, columns),
         hot.reshape(2 * n, 2, hot_rows, width),
-        outgoing, asked, table, accum,
+        outgoing, asked,
+        table.reshape(4, quarter, width),
+        accum.reshape(4, quarter, width),
     )
 
 
@@ -297,10 +315,18 @@
     matches = (owners[:, None] == jnp.arange(owners_count, dtype=jnp.int32)[None, :]).astype(
         jnp.int32
     )
-    earlier = jnp.cumsum(matches, axis=0) - matches
+    before = jnp.arange(lookups)[:, None] > jnp.arange(lookups)[None, :]
+    earlier = jnp.dot(
+        before.astype(jnp.bfloat16),
+        matches.astype(jnp.bfloat16),
+        preferred_element_type=jnp.float32,
+    ).astype(jnp.int32)
     positions = jnp.sum(earlier * matches, axis=1)
     targets = owners * capacity + positions
-    requests = jnp.zeros((owners_count * capacity,), jnp.int32).at[targets].set(cold_offset)
+    places = jnp.arange(owners_count * capacity, dtype=jnp.int32)
+    placed = targets[:, None] == places[None, :]
+    requests = jnp.sum(jnp.where(placed, cold_offset[:, None], 0), axis=0)
+    placed = placed.astype(jnp.bfloat16)
     requests = requests.reshape(owners_count, capacity)
     direct = suits(owners_count, lax.axis_size("rep"), top_weight.shape[0])
     if direct:
@@ -309,7 +335,11 @@
         asked = lax.all_to_all(requests, "dp", split_axis=0, concat_axis=0, tiled=True)
         found = cold_table[asked].astype(jnp.bfloat16)
         returned = lax.all_to_all(found, "dp", split_axis=0, concat_axis=0, tiled=True)
-    cold_rows = returned.reshape(owners_count * capacity, width)[targets]
+    cold_rows = jnp.dot(
+        placed,
+        returned.reshape(owners_count * capacity, width),
+        preferred_element_type=jnp.float32,
+    ).astype(jnp.bfloat16)
     cold_rows = cold_rows.reshape(samples, cold_feats, width)
     hot_rows = hot_cache[hot_ids].astype(jnp.bfloat16)
     inputs = jnp.concatenate([hot_rows, cold_rows], axis=1).reshape(
@@ -332,13 +362,12 @@
     ).astype(jnp.bfloat16)
     dinputs = dinputs.reshape(samples, hot_feats + cold_feats, width)
     cold_dx = dinputs[:, hot_feats:].reshape(lookups, width)
-    outgoing = jnp.zeros((owners_count * capacity, width), jnp.bfloat16).at[targets].set(cold_dx)
+    outgoing = lax.dot_general(
+        placed, cold_dx, (((0,), (0,)), ((), ())), preferred_element_type=jnp.float32
+    ).astype(jnp.bfloat16)
     outgoing = outgoing.reshape(owners_count, capacity, width)
     own_rows = cold_table.shape[0]
     quarter = own_rows // lax.axis_size("rep")
-    offset_rows = lax.axis_index("rep") * quarter
-    table_share = lax.dynamic_slice_in_dim(cold_table, offset_rows, quarter, 0)
-    accum_share = lax.dynamic_slice_in_dim(cold_accum, offset_rows, quarter, 0)
     hot_count = hot_cache.shape[0]
     blocks_count = hot_count // BLOCK
     hot_dx = dinputs[:, :hot_feats].reshape(samples * hot_feats, width)
@@ -348,11 +377,11 @@
     hot_grad = jnp.dot(hot_named, hot_dx, preferred_element_type=jnp.float32)
     carried = (pending + hot_grad).reshape(blocks_count, BLOCK, width)
     picked = carried[refresh_blocks]
-    divisors = 1.0 + block_clock[refresh_blocks].astype(jnp.float32)
+    divisors = 1.0 + block_clock.astype(jnp.float32)
+    named = refresh_blocks[:, None] == jnp.arange(blocks_count, dtype=jnp.int32)[None, :]
+    refreshed = jnp.any(named, axis=0)[:, None, None]
     cache_blocks = hot_cache.reshape(blocks_count, BLOCK, width)
     accum_blocks = hot_accum.reshape(blocks_count, BLOCK, width)
-    cache_chosen = cache_blocks[refresh_blocks]
-    accum_chosen = accum_blocks[refresh_blocks]
     if direct:
         picked_rows = refresh_blocks.shape[0] * BLOCK
         head_rows = head_term.shape[0] // width
@@ -366,7 +395,7 @@
             ]
         )
         top_grad, sums, cold_table_new, cold_accum_new = combine(
-            top_part, summands, outgoing, asked, table_share, accum_share
+            top_part, summands, outgoing, asked, cold_table, cold_accum
         )
         cold_table_new = cold_table_new.reshape(own_rows, width)
         cold_accum_new = cold_accum_new.reshape(own_rows, width)
@@ -381,6 +410,9 @@
             .add(incoming.reshape(-1, width).astype(jnp.float32))
         )
         cold_share = lax.psum_scatter(cold_grad, "rep", scatter_dimension=0, tiled=True)
+        offset_rows = lax.axis_index("rep") * quarter
+        table_share = lax.dynamic_slice_in_dim(cold_table, offset_rows, quarter, 0)
+        accum_share = lax.dynamic_slice_in_dim(cold_accum, offset_rows, quarter, 0)
         table_updated, accum_updated = adagrad(table_share, accum_share, cold_share)
         cold_table_new, cold_accum_new = (
             lax.all_gather(table_updated, "rep", axis=0, tiled=True),
@@ -388,11 +420,14 @@
         )
         top_grad = lax.psum_scatter(top_part, ("dp", "rep"), scatter_dimension=0, tiled=True)
         picked_sum, out_grad = lax.psum((picked, head_term), ("dp", "rep"))
-    flush = picked_sum / divisors[:, None, None]
-    cache_part, accum_part = adagrad(cache_chosen, accum_chosen, flush)
-    hot_cache_new = cache_blocks.at[refresh_blocks].set(cache_part).reshape(hot_count, width)
-    hot_accum_new = accum_blocks.at[refresh_blocks].set(accum_part).reshape(hot_count, width)
-    pending_new = carried.at[refresh_blocks].set(0.0).reshape(hot_count, width)
+    block_sums = jnp.zeros((), jnp.float32)
+    for k in range(refresh_blocks.shape[0]):
+        block_sums = jnp.where(named[k][:, None, None], picked_sum[k][None], block_sums)
+    flush = block_sums / divisors[:, None, None]
+    cache_next, accum_next = adagrad(cache_blocks, accum_blocks, flush)
+    hot_cache_new = jnp.where(refreshed, cache_next, cache_blocks).reshape(hot_count, width)
+    hot_accum_new = jnp.where(refreshed, accum_next, accum_blocks).reshape(hot_count, width)
+    pending_new = jnp.where(refreshed, 0.0, carried).reshape(hot_count, width)
     return (
         cold_table_new,
         cold_accum_new,

time: 92.6 us -> 77.8 us (0.84)
  local copies, waits for them, and re-layouts: 25.2 us -> 7.35 us
  Pallas kernels: 58 us -> 53.9 us
  matrix products: 4.57 us -> 8.51 us
  other arithmetic: 3.31 us -> 6.74 us
    scatter x5 -> x0, local copies, waits for them, and re-layouts: 8.45 us -> none  [the longest x1 3.17 us: local(): jnp.zeros((owners_count * capacity,), jnp.int32).at[targets]]
    pallas_call x1, Pallas kernels: 40.6 us -> 36.5 us  [combine(): pl.pallas_call(functools.partial(combine_kernel, n, links), out_shape=(ou...]
    dot_general x0 -> x3, matrix products: none -> 4.05 us  [the longest x1 1.52 us: local(): lax.dot_general(placed, cold_dx, (((0,), (0,)), ((), ())), preferred_elem...]
    unnamed x30 -> x29, local copies, waits for them, and re-layouts: 6.4 us -> 2.4 us
    gather x4 -> x0, local copies, waits for them, and re-layouts: 3.8 us -> none  [the longest x1 2.04 us: local(): cold_rows = returned.reshape(owners_count * capacity, width)[targets]]
    select_n x1, other arithmetic: 0.01 us -> 2.56 us  [local(): jnp.where(refreshed, accum_next, accum_blocks).reshape(hot_count, width)]
    dynamic_slice x1 -> x0, local copies, waits for them, and re-layouts: 1.53 us -> none  [local(): accum_share = lax.dynamic_slice_in_dim(cold_accum, offset_rows, quarter, 0)]
    reduce_sum x1, other arithmetic: 0.09 us -> 1.56 us  [local(): requests = jnp.sum(jnp.where(placed, cold_offset[:, None], 0), axis=0)]
where the time goes in v2:
time: 77.8 us; the launch traced here: 77.5 us
  Pallas kernels  53.9 us (69%)
  matrix products  8.51 us (11%)
  local copies, waits for them, and re-layouts  7.35 us (9%)
  other arithmetic  6.74 us (9%)
  between operations  0.91 us (1%)
    pallas_call x1, Pallas kernels, combine(): pl.pallas_call(functools.partial(combine_kernel, n, links), out_shape=(ou...  36.5 us
    pallas_call x1, Pallas kernels, fetch(): pl.pallas_call(functools.partial(fetch_kernel, n), out_shape=(jax.ShapeDt...  17.4 us
    select_n x1, other arithmetic, local(): jnp.where(refreshed, accum_next, accum_blocks).reshape(hot_count, width)  2.56 us
    unnamed x29, local copies, waits for them, and re-layouts  2.4 us
    dot_general x1, matrix products, local(): lax.dot_general(inputs, dhidden, (((0,), (0,)), ((), ())), preferred_elem...  2.07 us
    reduce_sum x1, other arithmetic, local(): requests = jnp.sum(jnp.where(placed, cold_offset[:, None], 0), axis=0)  1.56 us

profile of v2, /device:TPU:0, one launch (start us, length us, event | category | flops | bytes accessed | tf_op | source)
XLA Modules:
  0.0 77.5 jit_solution(2222635578375705994)
XLA Ops:
  0.7 1.1 %fusion.7 = s32[512]{0:T(512)S(1)} fusion(s32[512]{0:T(512)} %bitcast.122), kind=kOutput, calls=%fused_computation.14 | convolution fusion | flops 4484608 | bytes 4096 | tf_op jit(solution)/shard_map/dot_general | solution.py:319
  1.7 0.7 multiply_add_fusion.1
  2.4 1.6 %select_reduce_fusion = s32[1024]{0:T(1024)} fusion(s32[512]{0:T(512)} %param.15, s32[512]{0:T(512)S(1)} %bitcast.116), kind=kLoop, calls=%fused_computation.3 | loop fusion | flops 1571840 | bytes 8192 | tf_op jit(solution)/shard_map/reduce_sum | solution.py:328
  4.0 17.4 %shard_map.180 = (s32[8,1,128]{2,1,0:T(1,128)}, bf16[8,128,128]{2,1,0:T(8,128)(2,1)}) custom-call(s32[8,1,128]{2,1,0:T(1,128)} %bitcast.115, f32[512,128]{1,0:T(8,128)} %table.1), custom_call_target="tpu_custom_call" | custom-call | tf_op jit(solution)/shard_map/pallas_call | solution.py:88
  21.4 1.5 %fusion.5 = bf16[512,128]{1,0:T(8,128)(2,1)S(1)} fusion(bf16[1024,128]{1,0:T(8,128)(2,1)} %bitcast.124, s32[512]{0:T(512)S(1)} %bitcast.117), kind=kOutput, calls=%fused_computation.11 | convolution fusion | flops 134807552 | bytes 395264 | tf_op jit(solution)/shard_map/dot_general | solution.py:338
  22.9 0.7 compare_select_fusion
  23.9 1.1 %gather_fusion = bf16[512,128]{1,0:T(8,128)(2,1)S(1)} fusion(f32[1024,128]{1,0:T(8,128)S(1)} %copy-done.1, s32[1024]{0:T(1024)S(1)} %pad_clamp_fusion.1), kind=kCustom, calls=%fused_computation | custom fusion | bytes 264192 | tf_op jit(solution)/shard_map/gather | solution.py:344
  25.0 0.3 pad_maximum_fusion
  25.5 0.5 multiply_convert_fusion.1
  26.1 0.5 fusion.22
  26.7 2.1 %fusion.11.top = f32[16,2,16,1024]{3,2,1,0:T(8,128)} fusion(bf16[16,2,16,256]{3,2,1,0:T(8,128)(2,1)S(1)} %bitcast.107, f32[256,1024]{1,0:T(8,128)S(1)} %get-tuple-element.33, f32[1024]{0:T(1024)S(1)} %copy-done.8, f32[256]{0:T(256)S(1)} %divide_subtract_fusion), kind=kOutput, calls=%fused_computation.23 | convolution fusion | flops 271056896 | bytes 3412992 | tf_op jit(solution)/shard_map/dot_general | solution.py:357
  28.7 0.3 fusion.23
  29.1 0.6 convolution_convert_fusion
  30.3 0.5 fusion.3
  30.8 0.6 gather_fusion.1
  31.4 0.8 %maximum_maximum_fusion = f32[512,128]{1,0:T(8,128)} fusion(f32[8,128]{1,0:T(8,128)S(1)} %bitcast.114, f32[384,128]{1,0:T(8,128)S(1)} %bitcast.100, f32[512]{0:T(512)S(1)} %pad.2.clone), kind=kLoop, calls=%fused_computation.33 | loop fusion | flops 131072 | bytes 464896 | tf_op jit(solution)/shard_map/concatenate | solution.py:390
  32.3 1.5 %fusion.4 = bf16[1024,128]{1,0:T(8,128)(2,1)} fusion(bf16[512,128]{1,0:T(8,128)(2,1)S(1)} %bitcast.112, s32[512]{0:T(512)S(1)} %bitcast.118), kind=kOutput, calls=%fused_computation.9 | convolution fusion | flops 134873088 | bytes 395264 | tf_op jit(solution)/shard_map/dot_general | solution.py:365
  33.8 36.5 %shard_map.181 = (f32[16,1024]{1,0:T(8,128)}, f32[16,2,16,128]{3,2,1,0:T(8,128)}, f32[2,2,128,128]{3,2,1,0:T(8,128)}, f32[2,2,128,128]{3,2,1,0:T(8,128)}) custom-call(f32[16,2,16,1024]{3,2,1,0:T(8,128)} %fusion.11.top, f32[16,2,16,128]{3,2,1,0:T(8,128)} %bitcast.95, bf16[8,128,128]{2,1,0:T(8,128)(2,1)} %bitcast.104, s32[8,1,128]{2,1,0:T(1,128)} %get-tuple-element.14.asked, ...), custom_call_target="tpu_custom_call" | custom-call | tf_op jit(solution)/shard_map/pallas_call | solution.py:258
  70.4 1.0 %fusion.20 = (f32[4,2,16,128]{3,2,1,0:T(8,128)S(1)}, f32[4,2,16,128]{3,2,1,0:T(8,128)S(1)}, f32[4,2,16,128]{3,2,1,0:T(8,128)S(1)}) fusion(f32[16,2,16,128]{3,2,1,0:T(8,128)} %get-tuple-element.17), kind=kLoop, calls=%fused_computation.57 | loop fusion | bytes 393216 | tf_op jit(solution)/shard_map/slice | solution.py:425
  71.6 2.6 %fusion.16 = (f32[1024,128]{1,0:T(8,128)}, f32[1024,128]{1,0:T(8,128)}, f32[1024,128]{1,0:T(8,128)}) fusion(f32[1024,128]{1,0:T(8,128)S(1)} %copy-done.2, f32[1024]{0:T(1024)S(1)} %broadcast_bitcast_fusion, f32[128,128]{1,0:T(8,128)S(1)} %bitcast.109, f32[128,128]{1,0:T(8,128)S(1)} %bitcast.110, f32[128,128]{1,0:T(8,128)S(1)} %bitcast.108, ...), kind=kLoop, calls=%fused_computation.30 | loop fusion | flops 1703936 | bytes 3350528 | tf_op jit(solution)/shard_map/jit(_where)/select_n | solution.py:429
  74.2 1.3 %slice_bitcast_fusion = f32[1024]{0:T(1024)} fusion(f32[512,128]{1,0:T(8,128)} %bitcast.111), kind=kLoop, calls=%fused_computation.39 | loop fusion | bytes 8192 | tf_op jit(solution)/shard_map/reshape | solution.py:404
  75.4 0.7 copy.37
  76.1 0.7 copy.38
  76.8 0.6 copy.39
  (44 shorter events, 1.6 us)
Async XLA Ops:
  0.6 24.8 %copy-start = (bf16[512,1024]{1,0:T(8,128)(2,1)S(1)}, bf16[512,1024]{1,0:T(8,128)(2,1)}, u32[]{:S(2)}) copy-start(bf16[512,1024]{1,0:T(8,128)(2,1)} %param.17) | copy-start | bytes 3145732
  0.6 23.3 %copy-start.1 = (f32[1024,128]{1,0:T(8,128)S(1)}, f32[1024,128]{1,0:T(8,128)}, u32[]{:S(2)}) copy-start(f32[1024,128]{1,0:T(8,128)} %param.21) | copy-start | bytes 1572868
  25.5 0.7 copy-start.8
  25.5 1.2 %copy-start.9 = (s32[256]{0:T(256)S(1)}, s32[256]{0:T(256)}, u32[]{:S(2)}) copy-start(s32[256]{0:T(256)} %param.16) | copy-start | bytes 3076
  29.1 0.9 %copy-start.7 = (s32[256,2]{0,1:T(2,128)S(1)}, s32[256,2]{0,1:T(2,128)}, u32[]{:S(2)}) copy-start(s32[256,2]{0,1:T(2,128)} %param.13) | copy-start | bytes 6148
  29.1 1.2 %copy-start.3 = (f32[1024,128]{1,0:T(8,128)S(1)}, f32[1024,128]{1,0:T(8,128)}, u32[]{:S(2)}) copy-start(f32[1024,128]{1,0:T(8,128)} %param.23) | copy-start | bytes 1572868
  29.7 1.1 %copy-start.11 = (s32[3]{0:T(128)S(1)}, s32[3]{0:T(128)}, u32[]{:S(2)}) copy-start(s32[3]{0:T(128)} %param.24) | copy-start | bytes 40
  32.2 38.0 %copy-start.10 = (s32[8]{0:T(128)S(1)}, s32[8]{0:T(128)}, u32[]{:S(2)}) copy-start(s32[8]{0:T(128)} %param.25) | copy-start | bytes 100
  32.3 39.3 %copy-start.2 = (f32[1024,128]{1,0:T(8,128)S(1)}, f32[1024,128]{1,0:T(8,128)}, u32[]{:S(2)}) copy-start(f32[1024,128]{1,0:T(8,128)} %param.22) | copy-start | bytes 1572868
  70.3 5.1 %copy-start.5 = (f32[2,2,128,128]{3,2,1,0:T(8,128)S(1)}, f32[2,2,128,128]{3,2,1,0:T(8,128)}, u32[]{:S(2)}) copy-start(f32[2,2,128,128]{3,2,1,0:T(8,128)} %get-tuple-element.15) | copy-start | bytes 786436
  70.4 5.7 %copy-start.4 = (f32[2,2,128,128]{3,2,1,0:T(8,128)S(1)}, f32[2,2,128,128]{3,2,1,0:T(8,128)}, u32[]{:S(2)}) copy-start(f32[2,2,128,128]{3,2,1,0:T(8,128)} %get-tuple-element.16) | copy-start | bytes 786436
  71.6 5.2 %copy-start.6 = (f32[16,1024]{1,0:T(8,128)S(1)}, f32[16,1024]{1,0:T(8,128)}, u32[]{:S(2)}) copy-start(f32[16,1024]{1,0:T(8,128)} %get-tuple-element.50) | copy-start | bytes 196612
